TPU v7x, 32 devices: a whole 2x2x4 slice. The times are simulated.
32 devices in a mesh: dp: 16 (over z, y, x), seq: 2 (over core).
Axes of the slice: x: 2, y: 2, z: 4, core: 2. Of those that a mesh axis runs over, the one named last changes fastest.
Arguments:
- latents: float32 [16, 256, 48], P('dp', 'seq'), may hold values from -6 to 6
- valid: int32 [16, 256], P('dp', 'seq'), may hold values 0 or 1
- class_labels: int32 [16], replicated, may hold values from 0 to 447
- group_perm: int32 [16], P('dp'), may hold values from 0 to 15, as said below
- patch_weight: bfloat16 [48, 768], replicated, may hold values from -0.875 to 0.875
- pos_table: bfloat16 [256, 768], P('seq'), may hold values from -3 to 3
- class_table: bfloat16 [1024, 768], replicated, may hold values from -3 to 3
- ln1_gain: bfloat16 [1, 768], replicated, may hold values from 0.25 to 1.75
- ln1_bias: bfloat16 [1, 768], replicated, may hold values from -1.5 to 1.5
- qkv_weight: bfloat16 [1, 768, 2304], replicated, may hold values from -0.21875 to 0.21875
- out_weight: bfloat16 [1, 768, 768], replicated, may hold values from -0.875 to 0.875
- ln2_gain: bfloat16 [1, 768], replicated, may hold values from 0.25 to 1.75
- ln2_bias: bfloat16 [1, 768], replicated, may hold values from -1.5 to 1.5
- up_weight: bfloat16 [1, 768, 3072], replicated, may hold values from -0.21875 to 0.21875
- up_bias: bfloat16 [1, 3072], replicated, may hold values from -1.5 to 1.5
- down_weight: bfloat16 [1, 3072, 768], replicated, may hold values from -0.109375 to 0.109375
- head_weight: bfloat16 [768, 96], replicated, may hold values from -0.109375 to 0.109375
- head_bias: bfloat16 [96], replicated, may hold values from -1 to 1
- cot_latents: float32 [16, 256, 48], P('dp', 'seq'), may hold values from -6 to 6
- cot_logdet: float32 [16], P('dp'), may hold values from -4 to 4
Outputs:
- new_latents: float32 [16, 256, 48], P('dp', 'seq')
- logdet: float32 [16], P('dp')
- latents_grad: float32 [16, 256, 48], P('dp', 'seq')
- patch_weight_grad: float32 [48, 768], replicated
- pos_grad: float32 [256, 768], P('seq')
- class_grad: float32 [1024, 768], P('dp')
- ln1_gain_grad: float32 [1, 768], replicated
- ln1_bias_grad: float32 [1, 768], replicated
- qkv_grad: float32 [1, 768, 2304], replicated
- out_grad: float32 [1, 768, 768], replicated
- ln2_gain_grad: float32 [1, 768], replicated
- ln2_bias_grad: float32 [1, 768], replicated
- up_grad: float32 [1, 768, 3072], replicated
- up_bias_grad: float32 [1, 3072], replicated
- down_grad: float32 [1, 3072, 768], replicated
- head_weight_grad: float32 [768, 96], replicated
- head_bias_grad: float32 [96], replicated
Inputs may be any that keep to these rules, and one draw needn't show every extreme that they name: Each of 0 to 15 once; class_labels[group_perm] never falls.
All inputs are finite; a program needn't handle non-finite values. No bound on the sum of `valid` on one device may be relied on, other than what follows from the above.
Results may differ from a plain program's by a relative error of at most 0.023.
Values may be sent and summed in bfloat16 or wider, within the bound.
A program may use at most 320 MiB of HBM per device.

v0:
```python
import jax
import jax.numpy as jnp
from jax import lax
from jax.sharding import PartitionSpec as P

HEAD_DIM = 64
precise = lax.Precision.HIGHEST
norm_eps = 1e-05


def shifted_2(shard, axis, by):
    size = lax.axis_size(axis)
    pairs = [(i, i + by) for i in range(size) if 0 <= i + by < size]
    return lax.ppermute(shard, axis, pairs)


def layer_norm(values, norm_gain, norm_bias):
    center = values - jnp.mean(values, -1, keepdims=True)
    spread = jnp.mean(center * center, -1, keepdims=True)
    return center * lax.rsqrt(spread + norm_eps) * norm_gain + norm_bias


def matmul(left_side, weight_mat):
    return jnp.dot(left_side, weight_mat, preferred_element_type=jnp.float32)


def outer_sum(left_side, grad_side):
    left_flat = left_side.reshape(-1, left_side.shape[-1])
    grad_flat = grad_side.reshape(-1, grad_side.shape[-1])
    return lax.dot_general(
        left_flat, grad_flat, (((0,), (0,)), ((), ())), preferred_element_type=jnp.float32
    )


def transposed(grad_side, weight_mat):
    return lax.dot_general(
        grad_side,
        weight_mat,
        (((grad_side.ndim - 1,), (1,)), ((), ())),
        preferred_element_type=jnp.float32,
    )


def eight_rows(matrix):
    return matrix.reshape(8, -1)


def attention_mask(key_valid, patch_rows, seq_place):
    query_pos = seq_place * patch_rows + lax.iota(jnp.int32, patch_rows)
    key_pos = (seq_place - 1) * patch_rows + lax.iota(jnp.int32, 2 * patch_rows)
    earlier = (key_pos[None, :] < query_pos[:, None])[None] & (key_valid[:, None, :] > 0)
    return earlier | (key_pos[None, :] == query_pos[:, None])[None]


def masked_scores(query, keys, allowed):
    logits = jnp.einsum(
        "bqhd,bkhd->bhqk", query, keys, preferred_element_type=jnp.float32
    ) * HEAD_DIM ** (-0.5)
    return jnp.where(allowed[:, None], logits, -1e30)


def forward(latents, valid, class_rows, seq_place, weights):
    (
        patch_weight,
        pos_table,
        qkv_weight,
        out_weight,
        ln1_gain,
        ln1_bias,
        ln2_gain,
        ln2_bias,
        up_weight,
        up_bias,
        down_weight,
        head_weight,
        head_bias,
    ) = weights
    images, patch_rows, channels = latents.shape
    model_width = qkv_weight.shape[1]
    head_count = model_width // HEAD_DIM
    latent_low = latents.astype(jnp.bfloat16)
    hidden = (
        matmul(latent_low, patch_weight)
        + pos_table.astype(jnp.float32)[None]
        + class_rows[:, None, :]
    )
    own_mask = valid.astype(jnp.bfloat16)
    normed = layer_norm(
        hidden, ln1_gain[0].astype(jnp.float32), ln1_bias[0].astype(jnp.float32)
    ).astype(jnp.bfloat16)
    packed = matmul(normed, qkv_weight[0]).astype(jnp.bfloat16)
    query = packed[..., :model_width].reshape(images, patch_rows, head_count, HEAD_DIM)
    keys_own = packed[..., model_width : 2 * model_width]
    values_own = packed[..., 2 * model_width :]
    prior_keys, prior_values, prior_mask = shifted_2((keys_own, values_own, own_mask), "seq", 1)
    keys = jnp.concatenate((prior_keys, keys_own), 1).reshape(
        images, 2 * patch_rows, head_count, HEAD_DIM
    )
    values = jnp.concatenate((prior_values, values_own), 1).reshape(
        images, 2 * patch_rows, head_count, HEAD_DIM
    )
    allowed = attention_mask(jnp.concatenate((prior_mask, own_mask), 1), patch_rows, seq_place)
    logits = masked_scores(query, keys, allowed)
    row_peak = jnp.max(logits, -1, keepdims=True)
    log_total = row_peak + jnp.log(jnp.sum(jnp.exp(logits - row_peak), -1, keepdims=True))
    weights_soft = jnp.exp(logits - log_total).astype(jnp.bfloat16)
    attended = jnp.einsum(
        "bhqk,bkhd->bqhd", weights_soft, values, preferred_element_type=jnp.float32
    )
    attended = attended.astype(jnp.bfloat16).reshape(images, patch_rows, model_width)
    mid = hidden + matmul(attended, out_weight[0])
    second = layer_norm(
        mid, ln2_gain[0].astype(jnp.float32), ln2_bias[0].astype(jnp.float32)
    ).astype(jnp.bfloat16)
    preact = matmul(second, up_weight[0]) + up_bias[0].astype(jnp.float32)
    activated = jax.nn.gelu(preact, approximate=True).astype(jnp.bfloat16)
    saved = [
        (
            hidden,
            normed,
            query,
            keys,
            values,
            allowed,
            log_total,
            attended,
            mid,
            second,
            preact,
            activated,
        )
    ]
    hidden = mid + matmul(activated, down_weight[0])
    top_low = hidden.astype(jnp.bfloat16)
    head_out = matmul(top_low, head_weight) + head_bias.astype(jnp.float32)
    prior_row = shifted_2(head_out[:, patch_rows - 1, :], "seq", 1)
    shifted = jnp.concatenate((prior_row[:, None, :], head_out[:, : patch_rows - 1, :]), 1)
    shifted = shifted * valid.astype(jnp.float32)[..., None]
    alpha = shifted[..., :channels]
    shift_mean = shifted[..., channels:]
    factor = jnp.exp(-alpha)
    new_latents = (latents - shift_mean) * factor
    logdet_part = -jnp.sum(alpha, (1, 2))
    return (new_latents, logdet_part, factor, top_low, saved)


def local(
    latents,
    valid,
    class_labels,
    group_perm,
    patch_weight,
    pos_table,
    class_table,
    ln1_gain,
    ln1_bias,
    qkv_weight,
    out_weight,
    ln2_gain,
    ln2_bias,
    up_weight,
    up_bias,
    down_weight,
    head_weight,
    head_bias,
    cot_latents,
    cot_logdet,
):
    images, patch_rows, channels = latents.shape
    model_width = qkv_weight.shape[1]
    head_count = model_width // HEAD_DIM
    layer_total = qkv_weight.shape[0]
    seq_place = lax.axis_index("seq")
    picks = group_perm[:, None] == lax.iota(jnp.int32, class_labels.shape[0])[None, :]
    image_labels = jnp.sum(jnp.where(picks, class_labels[None, :], 0), 1)
    label_hot = image_labels[:, None] == lax.iota(jnp.int32, class_table.shape[0])[None, :]
    class_rows = matmul(label_hot.astype(jnp.bfloat16), class_table)
    weights = (
        patch_weight,
        pos_table,
        qkv_weight,
        out_weight,
        ln1_gain,
        ln1_bias,
        ln2_gain,
        ln2_bias,
        up_weight,
        up_bias,
        down_weight,
        head_weight,
        head_bias,
    )
    new_latents, logdet_part, factor, top_low, saved = forward(
        latents, valid, class_rows, seq_place, weights
    )
    latents_again, unused = lax.optimization_barrier((latents, new_latents))
    unused_a, unused_b, unused_c, unused_d, saved = forward(
        latents_again, valid, class_rows, seq_place, weights
    )
    valid_float = valid.astype(jnp.float32)
    d_alpha = -cot_latents * new_latents - cot_logdet[:, None, None]
    d_mean = -cot_latents * factor
    d_shifted = jnp.concatenate((d_alpha, d_mean), -1) * valid_float[..., None]
    next_row = shifted_2(d_shifted[:, 0, :], "seq", -1)
    d_head = jnp.concatenate((d_shifted[:, 1:, :], next_row[:, None, :]), 1).astype(jnp.bfloat16)
    head_weight_grad = outer_sum(top_low, d_head)
    head_bias_grad = jnp.sum(d_head.astype(jnp.float32), (0, 1))
    d_hidden = transposed(d_head, head_weight)
    grads_qkv, grads_out, grads_up, grads_down = ([], [], [], [])
    grads_g1, grads_b1, grads_g2, grads_b2, grads_ub = ([], [], [], [], [])
    for layer_index in reversed(range(layer_total)):
        (
            hidden,
            normed,
            query,
            keys,
            values,
            allowed,
            log_total,
            attended,
            mid,
            second,
            preact,
            activated,
        ) = saved[layer_index]
        d_down = d_hidden.astype(jnp.bfloat16)
        down_grad = outer_sum(activated, d_down)
        d_act = transposed(d_down, down_weight[layer_index])
        unused_gelu, gelu_pull = jax.vjp(lambda inner: jax.nn.gelu(inner, approximate=True), preact)
        d_pre = gelu_pull(d_act)[0].astype(jnp.bfloat16)
        up_bias_grad = jnp.sum(d_pre.astype(jnp.float32), (0, 1))
        up_grad = outer_sum(second, d_pre)
        d_second = transposed(d_pre, up_weight[layer_index])
        unused_norm, norm_pull = jax.vjp(
            layer_norm,
            mid,
            ln2_gain[layer_index].astype(jnp.float32),
            ln2_bias[layer_index].astype(jnp.float32),
        )
        d_mid_norm, ln2_gain_part, ln2_bias_part = norm_pull(d_second)
        d_mid = d_hidden + d_mid_norm
        d_proj = d_mid.astype(jnp.bfloat16)
        out_grad = outer_sum(attended, d_proj)
        d_attended = transposed(d_proj, out_weight[layer_index]).astype(jnp.bfloat16)
        d_attended = d_attended.reshape(images, patch_rows, head_count, HEAD_DIM)
        logits = masked_scores(query, keys, allowed)
        probs = jnp.exp(logits - log_total)
        d_probs = jnp.einsum(
            "bqhd,bkhd->bhqk", d_attended, values, preferred_element_type=jnp.float32
        )
        d_scores = (probs * (d_probs - jnp.sum(d_probs * probs, -1, keepdims=True))).astype(
            jnp.bfloat16
        )
        d_query = jnp.einsum(
            "bhqk,bkhd->bqhd", d_scores, keys, preferred_element_type=jnp.float32
        ) * HEAD_DIM ** (-0.5)
        d_keys = jnp.einsum(
            "bhqk,bqhd->bkhd", d_scores, query, preferred_element_type=jnp.float32
        ) * HEAD_DIM ** (-0.5)
        d_values = jnp.einsum(
            "bhqk,bqhd->bkhd",
            probs.astype(jnp.bfloat16),
            d_attended,
            preferred_element_type=jnp.float32,
        )
        d_keys = d_keys.reshape(images, 2 * patch_rows, model_width)
        d_values = d_values.reshape(images, 2 * patch_rows, model_width)
        back_keys, back_values = (
            shifted_2(d_keys[:, :patch_rows].astype(jnp.bfloat16), "seq", -1).astype(jnp.float32),
            shifted_2(d_values[:, :patch_rows].astype(jnp.bfloat16), "seq", -1).astype(jnp.float32),
        )
        d_packed = jnp.concatenate(
            (
                d_query.reshape(images, patch_rows, model_width),
                d_keys[:, patch_rows:] + back_keys,
                d_values[:, patch_rows:] + back_values,
            ),
            -1,
        ).astype(jnp.bfloat16)
        qkv_grad = outer_sum(normed, d_packed)
        d_normed = transposed(d_packed, qkv_weight[layer_index])
        unused_norm, norm_pull = jax.vjp(
            layer_norm,
            hidden,
            ln1_gain[layer_index].astype(jnp.float32),
            ln1_bias[layer_index].astype(jnp.float32),
        )
        d_input, ln1_gain_part, ln1_bias_part = norm_pull(d_normed)
        d_hidden = d_mid + d_input
        grads_qkv.insert(0, qkv_grad)
        grads_out.insert(0, out_grad)
        grads_up.insert(0, up_grad)
        grads_down.insert(0, down_grad)
        grads_g1.insert(0, ln1_gain_part)
        grads_b1.insert(0, ln1_bias_part)
        grads_g2.insert(0, ln2_gain_part)
        grads_b2.insert(0, ln2_bias_part)
        grads_ub.insert(0, up_bias_grad)
    d_embed_low = d_hidden.astype(jnp.bfloat16)
    patch_grad_part = outer_sum(latents.astype(jnp.bfloat16), d_embed_low)
    latents_grad = cot_latents * factor + transposed(d_embed_low, patch_weight)
    pos_part = jnp.sum(d_hidden, 0)
    class_part = jnp.sum(d_hidden, 1)
    logdet, class_sums = lax.psum((logdet_part, class_part), "seq")
    class_term = lax.dot_general(
        label_hot.astype(jnp.float32),
        class_sums,
        (((0,), (0,)), ((), ())),
        precision=precise,
        preferred_element_type=jnp.float32,
    )
    class_grad = lax.psum_scatter(class_term, "dp", scatter_dimension=0, tiled=True)
    pos_grad = lax.psum(pos_part, "dp")
    (
        patch_weight_grad,
        head_weight_grad,
        head_bias_grad,
        ln1_gain_grad,
        ln1_bias_grad,
        ln2_gain_grad,
        ln2_bias_grad,
        up_bias_grad,
    ) = lax.psum(
        (
            patch_grad_part,
            head_weight_grad,
            head_bias_grad,
            jnp.stack(grads_g1),
            jnp.stack(grads_b1),
            jnp.stack(grads_g2),
            jnp.stack(grads_b2),
            jnp.stack(grads_ub),
        ),
        ("dp", "seq"),
    )
    qkv_stack = jnp.stack(grads_qkv)
    out_stack = jnp.stack(grads_out)
    up_stack = jnp.stack(grads_up)
    down_stack = jnp.stack(grads_down)
    flat_parts = (
        lax.psum_scatter(eight_rows(qkv_stack), ("dp", "seq"), scatter_dimension=1, tiled=True),
        lax.psum_scatter(eight_rows(out_stack), ("dp", "seq"), scatter_dimension=1, tiled=True),
        lax.psum_scatter(eight_rows(up_stack), ("dp", "seq"), scatter_dimension=1, tiled=True),
        lax.psum_scatter(eight_rows(down_stack), ("dp", "seq"), scatter_dimension=1, tiled=True),
    )
    flat_qkv, flat_out, flat_up, flat_down = (
        lax.all_gather(
            flat_parts[0].astype(jnp.bfloat16), ("dp", "seq"), axis=1, tiled=True
        ).astype(jnp.float32),
        lax.all_gather(
            flat_parts[1].astype(jnp.bfloat16), ("dp", "seq"), axis=1, tiled=True
        ).astype(jnp.float32),
        lax.all_gather(
            flat_parts[2].astype(jnp.bfloat16), ("dp", "seq"), axis=1, tiled=True
        ).astype(jnp.float32),
        lax.all_gather(
            flat_parts[3].astype(jnp.bfloat16), ("dp", "seq"), axis=1, tiled=True
        ).astype(jnp.float32),
    )
    qkv_stack = flat_qkv.reshape(qkv_stack.shape)
    out_stack = flat_out.reshape(out_stack.shape)
    up_stack = flat_up.reshape(up_stack.shape)
    down_stack = flat_down.reshape(down_stack.shape)
    return (
        new_latents,
        logdet,
        latents_grad,
        patch_weight_grad,
        pos_grad,
        class_grad,
        ln1_gain_grad,
        ln1_bias_grad,
        qkv_stack,
        out_stack,
        ln2_gain_grad,
        ln2_bias_grad,
        up_stack,
        up_bias_grad,
        down_stack,
        head_weight_grad,
        head_bias_grad,
    )


def solution(mesh):
    in_specs = (
        P("dp", "seq", None),
        P("dp", "seq"),
        P(),
        P("dp"),
        P(),
        P("seq", None),
        P(),
        P(),
        P(),
        P(),
        P(),
        P(),
        P(),
        P(),
        P(),
        P(),
        P(),
        P(),
        P("dp", "seq", None),
        P("dp"),
    )
    out_specs = (
        P("dp", "seq", None),
        P("dp"),
        P("dp", "seq", None),
        P(),
        P("seq", None),
        P("dp", None),
        P(),
        P(),
        P(),
        P(),
        P(),
        P(),
        P(),
        P(),
        P(),
        P(),
        P(),
    )
    return jax.shard_map(local, mesh=mesh, in_specs=in_specs, out_specs=out_specs, check_vma=False)
```

profile of v0, /device:TPU:0, one launch (start us, length us, event | category | flops | bytes accessed | tf_op | source)
XLA Modules:
  0.0 1260.5 jit_solution(11902922079995836065)
XLA Ops:
  10.2 1.7 convolution_reduce_fusion
  14.1 3.0 collective-permute-start.2
  17.6 1.9 collective-permute-start.1
  19.5 2.0 collective-permute-start
  23.3 1.7 copy.52
  29.6 1.8 pad_maximum_fusion.2
  31.4 1.9 copy.53
  37.1 1.8 pad_maximum_fusion.1
  38.9 1.9 copy.51
  40.9 2.1 convolution_convert_fusion.3
  44.9 6.5 fusion.57
  57.1 2.0 multiply_subtract_fusion
  64.6 2.9 collective-permute-start.6
  68.8 1.7 copy.57
  70.5 4.3 collective-permute-start.5
  74.8 2.0 fusion.109
  76.8 1.8 pad_maximum_fusion.4
  78.6 1.9 copy.58
  80.6 1.6 fusion.136
  83.9 1.7 pad_maximum_fusion.3
  85.6 1.9 copy.56
  87.5 2.1 convolution_convert_fusion.2
  90.4 3.3 fusion.13
  93.8 5.5 convert_reduce_fusion
  99.3 2.3 multiply_reduce_fusion.1
  102.7 1.9 fusion.96
  104.6 3.5 reshape_stack.13
  108.2 2.6 fusion.60
  110.8 1.7 copy.59
  112.5 2.5 multiply_reduce_fusion
  120.2 1.6 collective-permute-done.8
  122.5 4.2 fusion.76
  126.7 7.2 reshape_stack.12
  134.6 6.5 fusion.125
  141.1 9.2 reshape_stack.14
  150.4 6.8 fusion.66
  157.2 9.3 reshape_stack.15
  166.6 42.8 %reduce-scatter.10.cloned.1.call-done = f32[8,2304]{1,0:T(8,128)} async-done(((f32[8,73728]{1,0:T(8,128)}), f32[8,2304]{1,0:T(8,128)}) %reduce-scatter.10.cloned.1.call-update) | async-done | bytes 73744 | tf_op jit(solution)/shard_map/reduce_scatter | solution.py:342
  211.0 123.2 %reduce-scatter.8.cloned.1.call-done = f32[8,6912]{1,0:T(8,128)} async-done(((f32[8,221184]{1,0:T(8,128)}), f32[8,6912]{1,0:T(8,128)}) %reduce-scatter.8.cloned.1.call-update) | async-done | bytes 221200 | tf_op jit(solution)/shard_map/reduce_scatter | solution.py:341
  334.2 1.6 convert_element_type.273
  335.8 139.6 %reduce-scatter.12.cloned.1.call-done = f32[8,9216]{1,0:T(8,128)} async-done(((f32[8,294912]{1,0:T(8,128)}), f32[8,9216]{1,0:T(8,128)}) %reduce-scatter.12.cloned.1.call-update) | async-done | bytes 294928 | tf_op jit(solution)/shard_map/reduce_scatter | solution.py:343
  475.4 1.6 convert_element_type.275
  477.1 139.7 %reduce-scatter.14.cloned.1.call-done = f32[8,9216]{1,0:T(8,128)} async-done(((f32[8,294912]{1,0:T(8,128)}), f32[8,9216]{1,0:T(8,128)}) %reduce-scatter.14.cloned.1.call-update) | async-done | bytes 294928 | tf_op jit(solution)/shard_map/reduce_scatter | solution.py:344
  616.8 1.6 convert_element_type.278
  618.5 1.9 fusion.108
  620.5 3.4 multiply_reduce_fusion.2
  624.9 1.8 convolution_bitcast_fusion
  626.8 1.9 fusion.65
  630.6 3.6 all-reduce.2
  634.2 1.9 broadcast_multiply_fusion
  639.2 41.3 %all-reduce = (f32[1,768]{1,0:T(1,128)}, f32[1,768]{1,0:T(1,128)}, f32[1,768]{1,0:T(1,128)}, f32[1,768]{1,0:T(1,128)}, f32[1,3072]{1,0:T(1,128)}, /*index=5*/f32[96]{0:T(128)}) all-reduce(f32[1,768]{1,0:T(1,128)S(1)} %stack.15, f32[1,768]{1,0:T(1,128)S(1)} %stack.16, ...), channel_id=1, replica_groups=mesh['dp'=16,'seq'=2] {'dp','seq'}, use_global_device_ids=true, to_apply=%region_26.27 | all-reduce | flops 6240 | bytes 49920 | tf_op jit(solution)/shard_map/psum | solution.py:323
  680.5 3.1 reshape.960
  683.6 51.8 %all-gather.5.cloned.1.call-done = bf16[8,221184]{1,0:T(8,128)(2,1)} async-done(((bf16[8,6912]{1,0:T(8,128)(2,1)}), bf16[8,221184]{1,0:T(8,128)(2,1)}) %all-gather.5.cloned.1.call-update) | async-done | bytes 3538960 | tf_op jit(solution)/shard_map/all_gather | solution.py:347
  735.4 6.3 reshape.958
  741.8 59.6 %all-gather.9.cloned.1.call-done = bf16[8,294912]{1,0:T(8,128)(2,1)} async-done(((bf16[8,9216]{1,0:T(8,128)(2,1)}), bf16[8,294912]{1,0:T(8,128)(2,1)}) %all-gather.9.cloned.1.call-update) | async-done | bytes 4718608 | tf_op jit(solution)/shard_map/all_gather | solution.py:353
  801.4 7.9 reshape.962
  809.3 57.4 %all-gather.11.cloned.1.call-done = bf16[8,294912]{1,0:T(8,128)(2,1)} async-done(((bf16[8,9216]{1,0:T(8,128)(2,1)}), bf16[8,294912]{1,0:T(8,128)(2,1)}) %all-gather.11.cloned.1.call-update) | async-done | bytes 4718608 | tf_op jit(solution)/shard_map/all_gather | solution.py:356
  866.7 7.9 reshape.964
  874.6 123.7 %all-reduce.8.cloned.1.call-done = (f32[48,768]{1,0:T(8,128)}, f32[768,96]{0,1:T(8,128)}) async-done(((f32[48,768]{1,0:T(8,128)}, f32[768,96]{0,1:T(8,128)}), (f32[48,768]{1,0:T(8,128)}, f32[768,96]{0,1:T(8,128)})) %all-reduce.8.cloned.1.call-update) | async-done | bytes 442384 | tf_op jit(solution)/shard_map/psum | solution.py:323
  998.3 115.3 %all-reduce.6.cloned.1.call-done = f32[128,768]{1,0:T(8,128)} async-done(((f32[128,768]{1,0:T(8,128)}), f32[128,768]{1,0:T(8,128)}) %all-reduce.6.cloned.1.call-update) | async-done | bytes 393232 | tf_op jit(solution)/shard_map/psum | solution.py:313
  1113.7 135.2 %reduce-scatter.6.cloned.1.call-done = f32[64,768]{1,0:T(8,128)} async-done(((f32[1024,768]{1,0:T(8,128)}), f32[64,768]{1,0:T(8,128)}) %reduce-scatter.6.cloned.1.call-update) | async-done | bytes 196624 | tf_op jit(solution)/shard_map/reduce_scatter | solution.py:312
  1248.9 1.6 copy.66
  1250.5 1.8 copy.67
  1252.3 1.7 copy.68
  (220 shorter events, 45.8 us)
Async XLA Ops:
  7.2 5.4 copy-start
  7.2 5.3 copy-start.51
  7.2 5.3 copy-start.50
  7.2 202.2 %reduce-scatter.10.cloned.1.call-start = ((), (), s32[]{:S(2)}) async-start(), calls=%async_computation.9 | async-start | bytes 2433024 | tf_op jit(solution)/shard_map/reduce_scatter | solution.py:342
  7.3 4.6 copy-start.23
  7.3 4.6 copy-start.27
  7.3 4.6 copy-start.29
  12.5 50.5 %copy-start.32 = (f32[768]{0:T(1024)}, f32[768]{0:T(1024)S(1)}, u32[]{:S(2)}) copy-start(f32[768]{0:T(1024)S(1)} %get-tuple-element.71) | copy-start | bytes 9220
  12.6 4.6 copy-start.55
  14.1 15.5 %collective-permute-start.2 = (bf16[1,128,768]{2,1,0:T(8,128)(2,1)}, bf16[1,128,768]{2,1,0:T(8,128)(2,1)}, u32[]{:S(2)}, u32[]{:S(2)}) collective-permute-start(bf16[1,128,768]{2,1,0:T(8,128)(2,1)} %get-tuple-element.46), channel_id=1, source_target_pairs={{0,1},{2,3},{4,5},{6,7},{8,9},{10,11},{12,13},{14,15},{16,17},{18,... | collective-permute-start | bytes 589832 | tf_op jit(solution)/shard_map/ppermute | solution.py:14
  17.6 9.9 collective-permute-start.1
  19.5 17.6 %collective-permute-start = (bf16[1,128,768]{2,1,0:T(8,128)(2,1)}, bf16[1,128,768]{2,1,0:T(8,128)(2,1)}, u32[]{:S(2)}, u32[]{:S(2)}) collective-permute-start(bf16[1,128,768]{2,1,0:T(8,128)(2,1)} %get-tuple-element.48), channel_id=1, source_target_pairs={{0,1},{2,3},{4,5},{6,7},{8,9},{10,11},{12,13},{14,15},{16,17},{18,... | collective-permute-start | bytes 589832 | tf_op jit(solution)/shard_map/ppermute | solution.py:14
  23.3 21.6 %copy-start.34 = (f32[768]{0:T(1024)}, f32[768]{0:T(1024)S(1)}, u32[]{:S(2)}) copy-start(f32[768]{0:T(1024)S(1)} %get-tuple-element.73) | copy-start | bytes 9220
  34.9 1.1 copy-start.8
  40.8 2.1 copy-start.9
  40.9 2.1 copy-start.13
  53.3 2.1 collective-permute-start.3
  57.1 2.0 copy-start.31
  59.7 2.8 copy-start.30
  62.3 1.5 copy-start.3
  62.4 1.4 copy-start.43
  64.6 12.2 collective-permute-start.6
  67.5 7.3 collective-permute-start.4
  70.5 13.3 %collective-permute-start.5 = (bf16[1,128,768]{2,1,0:T(8,128)(2,1)}, bf16[1,128,768]{2,1,0:T(8,128)(2,1)}, u32[]{:S(2)}, u32[]{:S(2)}) collective-permute-start(bf16[1,128,768]{2,1,0:T(8,128)(2,1)} %get-tuple-element.45), channel_id=1, source_target_pairs={{0,1},{2,3},{4,5},{6,7},{8,9},{10,11},{12,13},{14,15},{16,17},{18,... | collective-permute-start | bytes 589832 | tf_op jit(solution)/shard_map/ppermute | solution.py:14
  80.6 3.3 copy-start.22
  82.2 1.1 copy-start.1
  87.5 2.2 copy-start.4
  87.5 2.2 copy-start.10
  90.1 11.5 copy-start.7
  90.1 11.5 copy-start.39
  90.4 11.3 copy-start.46
  90.4 3.4 copy-start.17
  90.4 8.9 slice-start
  93.8 5.5 copy-start.11
  93.8 5.5 slice-start.1
  99.3 2.3 copy-start.18
  108.1 226.0 %reduce-scatter.8.cloned.1.call-start = ((), (), s32[]{:S(2)}) async-start(), calls=%async_computation.7 | async-start | bytes 7299072 | tf_op jit(solution)/shard_map/reduce_scatter | solution.py:341
  112.5 2.5 copy-start.2
  116.0 1.8 copy-start.19
  116.3 3.4 copy-start.16
  116.3 3.9 collective-permute-start.7
  118.3 4.3 copy-start.5
  118.3 4.3 copy-start.33
  118.3 4.2 copy-start.44
  118.3 4.2 copy-start.48
  118.3 3.5 collective-permute-start.8
  120.1 1.7 copy-start.26
  120.2 1.6 copy-start.24
  133.9 341.5 %reduce-scatter.12.cloned.1.call-start = ((), (), s32[]{:S(2)}) async-start(), calls=%async_computation.11 | async-start | bytes 9732096 | tf_op jit(solution)/shard_map/reduce_scatter | solution.py:343
  150.4 466.4 %reduce-scatter.14.cloned.1.call-start = ((), (), s32[]{:S(2)}) async-start(), calls=%async_computation.13 | async-start | bytes 9732096 | tf_op jit(solution)/shard_map/reduce_scatter | solution.py:344
  166.5 453.9 %copy-start.45 = (f32[128]{0:T(128)S(1)}, f32[128]{0:T(128)}, u32[]{:S(2)}) copy-start(f32[128]{0:T(128)} %copy-done.43) | copy-start | bytes 1540
  166.5 453.9 %copy-start.49 = (f32[128]{0:T(128)S(1)}, f32[128]{0:T(128)}, u32[]{:S(2)}) copy-start(f32[128]{0:T(128)} %copy-done.47) | copy-start | bytes 1540
  166.6 513.9 %all-gather.7.cloned.1.call-start = ((), (), s32[]{:S(2)}) async-start(), calls=%async_computation.10 | async-start | bytes 1216512 | tf_op jit(solution)/shard_map/all_gather | solution.py:350
  210.9 524.5 %all-gather.5.cloned.1.call-start = ((), (), s32[]{:S(2)}) async-start(), calls=%async_computation.8 | async-start | bytes 3649536 | tf_op jit(solution)/shard_map/all_gather | solution.py:347
  335.8 465.6 %all-gather.9.cloned.1.call-start = ((), (), s32[]{:S(2)}) async-start(), calls=%async_computation.12 | async-start | bytes 4866048 | tf_op jit(solution)/shard_map/all_gather | solution.py:353
  477.1 389.6 %all-gather.11.cloned.1.call-start = ((), (), s32[]{:S(2)}) async-start(), calls=%async_computation.14 | async-start | bytes 4866048 | tf_op jit(solution)/shard_map/all_gather | solution.py:356
  618.5 379.9 %all-reduce.8.cloned.1.call-start = ((), (), s32[]{:S(2)}) async-start(), calls=%async_computation.15 | async-start | bytes 884736 | tf_op jit(solution)/shard_map/psum | solution.py:323
  620.4 3.4 copy-start.53
  620.4 3.4 copy-start.6
  620.4 3.6 copy-start.15
  628.7 485.0 %all-reduce.6.cloned.1.call-start = ((), (), s32[]{:S(2)}) async-start(), calls=%async_computation.5 | async-start | bytes 786432 | tf_op jit(solution)/shard_map/psum | solution.py:313
  629.2 619.7 %reduce-scatter.6.cloned.1.call-start = ((), (), s32[]{:S(2)}) async-start(), calls=%async_computation.6 | async-start | bytes 3342336 | tf_op jit(solution)/shard_map/reduce_scatter | solution.py:312
  636.2 2.3 copy-start.42
  636.2 2.3 copy-start.41
  (14 other events, 10.3 us)
Sparse Core Ops, SparseCore 0:
  108.3 101.0 reduce-scatter.9
  216.0 118.1 reduce-scatter.7
  340.6 134.7 reduce-scatter.11
  482.2 134.5 reduce-scatter.13
  619.6 53.5 all-gather.6
  676.5 58.9 all-gather.4
  738.9 62.4 all-gather.8
  804.3 62.4 all-gather.10
  873.2 125.0 all-reduce.7
  1004.8 108.8 all-reduce.5
  1119.2 129.6 reduce-scatter.5
where the time goes:
time: 1260 us
  waiting for transfers between devices  991 us (79%)
  local copies, waits for them, and re-layouts  84.4 us (7%)
  matrix products  68.3 us (5%)
  blocking collectives  44.9 us (4%)
  other arithmetic  34.9 us (3%)
  starting transfers between devices  20.1 us (2%)
  between operations  17 us (1%)
    reduce_scatter x1, waiting for transfers between devices, local(): lax.psum_scatter(eight_rows(down_stack), ('dp', 'seq'), scatter_dimension...  140 us
    reduce_scatter x1, waiting for transfers between devices, local(): lax.psum_scatter(eight_rows(up_stack), ('dp', 'seq'), scatter_dimension=1...  140 us
    reduce_scatter x1, waiting for transfers between devices, local(): lax.psum_scatter(class_term, 'dp', scatter_dimension=0, tiled=True)  135 us
    psum x1, waiting for transfers between devices, local(): lax.psum((patch_grad_part, head_weight_grad, head_bias_grad, jnp.stack(gr...  124 us
    reduce_scatter x1, waiting for transfers between devices, local(): lax.psum_scatter(eight_rows(qkv_stack), ('dp', 'seq'), scatter_dimension=...  123 us
    psum x1, waiting for transfers between devices, local(): pos_grad = lax.psum(pos_part, 'dp')  115 us
    all_gather x1, waiting for transfers between devices, local(): lax.all_gather(flat_parts[2].astype(jnp.bfloat16), ('dp', 'seq'), axis=1,...  59.6 us
    all_gather x1, waiting for transfers between devices, local(): lax.all_gather(flat_parts[3].astype(jnp.bfloat16), ('dp', 'seq'), axis=1,...  57.4 us
  transfers between devices with their start and end apart: 20, of which 12 were waited for; matrix products, arithmetic and copies ran while one was open for 10% of the time, Pallas kernels for 0%

commit v1 on v0

--- a/solution.py
+++ b/solution.py
@@ -310,7 +310,9 @@
         preferred_element_type=jnp.float32,
     )
     class_grad = lax.psum_scatter(class_term, "dp", scatter_dimension=0, tiled=True)
-    pos_grad = lax.psum(pos_part, "dp")
+    pos_grad = pos_part
+    for hop in (1, 2, 4, 8):
+        pos_grad = pos_grad + lax.ppermute(pos_grad, "dp", [(dev, dev ^ hop) for dev in range(16)])
     (
         patch_weight_grad,
         head_weight_grad,

time: 1260 us -> 1030 us (0.82)
  waiting for transfers between devices: 991 us -> 739 us
    reduce_scatter x1, waiting for transfers between devices: 135 us -> 0.01 us  [local(): lax.psum_scatter(class_term, 'dp', scatter_dimension=0, tiled=True)]
    psum x1 -> x0, waiting for transfers between devices: 115 us -> none  [local(): pos_grad = lax.psum(pos_part, 'dp')]
    all_gather x1, waiting for transfers between devices: 51.8 us -> 9.61 us  [local(): lax.all_gather(flat_parts[0].astype(jnp.bfloat16), ('dp', 'seq'), axis=1,...]
    ppermute x0 -> x4, waiting for transfers between devices: none -> 36.2 us  [local(): lax.ppermute(pos_grad, 'dp', [(dev, dev ^ hop) for dev in range(16)])]
  transfers between devices with their start and end apart: 20 -> 23, of which waited for: 12 -> 13; matrix products, arithmetic and copies ran while one was open for 10% -> 12% of each run, Pallas kernels for 0% -> 0%
where the time goes in v1:
time: 1030 us; the launch traced here: 1020 us
  waiting for transfers between devices  739 us (72%)
  local copies, waits for them, and re-layouts  81.1 us (8%)
  matrix products  68.3 us (7%)
  blocking collectives  47.3 us (5%)
  other arithmetic  38.7 us (4%)
  starting transfers between devices  28.3 us (3%)
  between operations  18.7 us (2%)
    reduce_scatter x1, waiting for transfers between devices, local(): lax.psum_scatter(eight_rows(down_stack), ('dp', 'seq'), scatter_dimension...  140 us
    reduce_scatter x1, waiting for transfers between devices, local(): lax.psum_scatter(eight_rows(up_stack), ('dp', 'seq'), scatter_dimension=1...  140 us
    psum x1, waiting for transfers between devices, local(): lax.psum((patch_grad_part, head_weight_grad, head_bias_grad, jnp.stack(gr...  124 us
    reduce_scatter x1, waiting for transfers between devices, local(): lax.psum_scatter(eight_rows(qkv_stack), ('dp', 'seq'), scatter_dimension=...  123 us
    all_gather x1, waiting for transfers between devices, local(): lax.all_gather(flat_parts[2].astype(jnp.bfloat16), ('dp', 'seq'), axis=1,...  64.7 us
    all_gather x1, waiting for transfers between devices, local(): lax.all_gather(flat_parts[3].astype(jnp.bfloat16), ('dp', 'seq'), axis=1,...  57.5 us
    psum x1, blocking collectives, local(): lax.psum((patch_grad_part, head_weight_grad, head_bias_grad, jnp.stack(gr...  43.6 us
    reduce_scatter x1, waiting for transfers between devices, local(): lax.psum_scatter(eight_rows(out_stack), ('dp', 'seq'), scatter_dimension=...  42.8 us
  transfers between devices with their start and end apart: 23, of which 13 were waited for; matrix products, arithmetic and copies ran while one was open for 12% of the time, Pallas kernels for 0%

profile of v1, /device:TPU:0, one launch (start us, length us, event | category | flops | bytes accessed | tf_op | source)
XLA Modules:
  0.0 1021.4 jit_solution(17994506605280541815)
XLA Ops:
  11.0 1.7 convolution_reduce_fusion
  14.9 3.0 collective-permute-start.2
  18.5 1.8 collective-permute-start.1
  20.3 2.0 collective-permute-start
  24.1 1.7 copy.52
  30.4 1.8 pad_maximum_fusion.2
  32.2 1.9 copy.53
  37.9 1.8 pad_maximum_fusion.1
  39.7 1.9 copy.51
  41.6 2.1 convolution_convert_fusion.3
  45.6 6.5 fusion.57
  57.9 2.0 multiply_subtract_fusion
  65.4 2.9 collective-permute-start.6
  69.6 1.7 copy.57
  71.3 4.5 collective-permute-start.5
  75.9 2.0 fusion.109
  77.9 1.8 pad_maximum_fusion.4
  79.7 1.9 copy.58
  81.6 1.6 fusion.136
  84.9 1.7 pad_maximum_fusion.3
  86.6 1.9 copy.56
  88.5 2.1 convolution_convert_fusion.2
  91.4 3.3 fusion.13
  94.8 5.5 convert_reduce_fusion
  100.3 2.3 multiply_reduce_fusion.1
  103.8 1.9 fusion.96
  105.6 3.5 reshape_stack.13
  109.2 2.6 fusion.60
  111.8 1.7 copy.59
  113.6 2.5 multiply_reduce_fusion
  123.6 4.2 fusion.76
  127.7 7.2 reshape_stack.12
  135.6 6.5 fusion.125
  142.2 9.2 reshape_stack.14
  151.4 6.8 fusion.66
  158.2 9.3 reshape_stack.15
  167.6 42.8 %reduce-scatter.10.cloned.1.call-done = f32[8,2304]{1,0:T(8,128)} async-done(((f32[8,73728]{1,0:T(8,128)}), f32[8,2304]{1,0:T(8,128)}) %reduce-scatter.10.cloned.1.call-update) | async-done | bytes 73744 | tf_op jit(solution)/shard_map/reduce_scatter | solution.py:344
  212.0 123.3 %reduce-scatter.8.cloned.1.call-done = f32[8,6912]{1,0:T(8,128)} async-done(((f32[8,221184]{1,0:T(8,128)}), f32[8,6912]{1,0:T(8,128)}) %reduce-scatter.8.cloned.1.call-update) | async-done | bytes 221200 | tf_op jit(solution)/shard_map/reduce_scatter | solution.py:343
  335.2 1.6 convert_element_type.273
  336.9 139.6 %reduce-scatter.12.cloned.1.call-done = f32[8,9216]{1,0:T(8,128)} async-done(((f32[8,294912]{1,0:T(8,128)}), f32[8,9216]{1,0:T(8,128)}) %reduce-scatter.12.cloned.1.call-update) | async-done | bytes 294928 | tf_op jit(solution)/shard_map/reduce_scatter | solution.py:345
  476.5 1.6 convert_element_type.275
  478.2 139.8 %reduce-scatter.14.cloned.1.call-done = f32[8,9216]{1,0:T(8,128)} async-done(((f32[8,294912]{1,0:T(8,128)}), f32[8,9216]{1,0:T(8,128)}) %reduce-scatter.14.cloned.1.call-update) | async-done | bytes 294928 | tf_op jit(solution)/shard_map/reduce_scatter | solution.py:346
  618.0 1.6 convert_element_type.278
  621.0 1.9 fusion.108
  623.0 3.4 multiply_reduce_fusion.2
  627.5 3.6 all-reduce.2
  631.1 1.8 convolution_bitcast_fusion
  633.0 1.9 broadcast_multiply_fusion
  636.5 10.3 %collective-permute-done.9 = f32[128,768]{1,0:T(8,128)S(1)} collective-permute-done((f32[128,768]{1,0:T(8,128)}, f32[128,768]{1,0:T(8,128)S(1)}, u32[]{:S(2)}, u32[]{:S(2)}) %collective-permute-start.9) | collective-permute-done | bytes 393248 | tf_op jit(solution)/shard_map/ppermute | solution.py:315
  649.0 9.2 collective-permute-done.10
  659.9 16.7 %collective-permute-done.11 = f32[128,768]{1,0:T(8,128)S(1)} collective-permute-done((f32[128,768]{1,0:T(8,128)S(1)}, f32[128,768]{1,0:T(8,128)S(1)}, u32[]{:S(2)}, u32[]{:S(2)}) %collective-permute-start.11) | collective-permute-done | bytes 393248 | tf_op jit(solution)/shard_map/ppermute | solution.py:315
  677.3 3.6 collective-permute-start.12
  682.5 43.6 %all-reduce = (f32[1,768]{1,0:T(1,128)}, f32[1,768]{1,0:T(1,128)}, f32[1,768]{1,0:T(1,128)}, f32[1,768]{1,0:T(1,128)}, f32[1,3072]{1,0:T(1,128)}, /*index=5*/f32[96]{0:T(128)}) all-reduce(f32[1,768]{1,0:T(1,128)S(1)} %stack.15, f32[1,768]{1,0:T(1,128)S(1)} %stack.16, ...), channel_id=1, replica_groups=mesh['dp'=16,'seq'=2] {'dp','seq'}, use_global_device_ids=true, to_apply=%region_25.26 | all-reduce | flops 6240 | bytes 49920 | tf_op jit(solution)/shard_map/psum | solution.py:325
  726.2 1.9 fusion.65
  728.0 1.9 add.296
  729.9 3.1 reshape.960
  733.1 9.6 all-gather.5.cloned.1.call-done
  742.7 6.3 reshape.958
  749.0 64.7 %all-gather.9.cloned.1.call-done = bf16[8,294912]{1,0:T(8,128)(2,1)} async-done(((bf16[8,9216]{1,0:T(8,128)(2,1)}), bf16[8,294912]{1,0:T(8,128)(2,1)}) %all-gather.9.cloned.1.call-update) | async-done | bytes 4718608 | tf_op jit(solution)/shard_map/all_gather | solution.py:355
  813.8 7.9 reshape.962
  821.7 57.5 %all-gather.11.cloned.1.call-done = bf16[8,294912]{1,0:T(8,128)(2,1)} async-done(((bf16[8,9216]{1,0:T(8,128)(2,1)}), bf16[8,294912]{1,0:T(8,128)(2,1)}) %all-gather.11.cloned.1.call-update) | async-done | bytes 4718608 | tf_op jit(solution)/shard_map/all_gather | solution.py:358
  879.1 7.9 reshape.964
  887.0 123.7 %all-reduce.5.cloned.1.call-done = (f32[48,768]{1,0:T(8,128)}, f32[768,96]{0,1:T(8,128)}) async-done(((f32[48,768]{1,0:T(8,128)}, f32[768,96]{0,1:T(8,128)}), (f32[48,768]{1,0:T(8,128)}, f32[768,96]{0,1:T(8,128)})) %all-reduce.5.cloned.1.call-update) | async-done | bytes 442384 | tf_op jit(solution)/shard_map/psum | solution.py:325
  1012.4 1.7 copy.66
  (234 shorter events, 53.0 us)
Async XLA Ops:
  8.0 5.4 copy-start
  8.0 5.3 copy-start.54
  8.0 5.3 copy-start.53
  8.1 202.4 %reduce-scatter.10.cloned.1.call-start = ((), (), s32[]{:S(2)}) async-start(), calls=%async_computation.8 | async-start | bytes 2433024 | tf_op jit(solution)/shard_map/reduce_scatter | solution.py:344
  8.1 4.6 copy-start.23
  8.1 4.6 copy-start.27
  8.1 4.6 copy-start.29
  13.4 50.5 %copy-start.33 = (f32[768]{0:T(1024)}, f32[768]{0:T(1024)S(1)}, u32[]{:S(2)}) copy-start(f32[768]{0:T(1024)S(1)} %get-tuple-element.71) | copy-start | bytes 9220
  13.4 4.6 copy-start.58
  14.9 15.5 %collective-permute-start.2 = (bf16[1,128,768]{2,1,0:T(8,128)(2,1)}, bf16[1,128,768]{2,1,0:T(8,128)(2,1)}, u32[]{:S(2)}, u32[]{:S(2)}) collective-permute-start(bf16[1,128,768]{2,1,0:T(8,128)(2,1)} %get-tuple-element.46), channel_id=1, source_target_pairs={{0,1},{2,3},{4,5},{6,7},{8,9},{10,11},{12,13},{14,15},{16,17},{18,... | collective-permute-start | bytes 589832 | tf_op jit(solution)/shard_map/ppermute | solution.py:14
  18.5 9.8 collective-permute-start.1
  20.3 17.6 %collective-permute-start = (bf16[1,128,768]{2,1,0:T(8,128)(2,1)}, bf16[1,128,768]{2,1,0:T(8,128)(2,1)}, u32[]{:S(2)}, u32[]{:S(2)}) collective-permute-start(bf16[1,128,768]{2,1,0:T(8,128)(2,1)} %get-tuple-element.48), channel_id=1, source_target_pairs={{0,1},{2,3},{4,5},{6,7},{8,9},{10,11},{12,13},{14,15},{16,17},{18,... | collective-permute-start | bytes 589832 | tf_op jit(solution)/shard_map/ppermute | solution.py:14
  24.1 21.6 %copy-start.35 = (f32[768]{0:T(1024)}, f32[768]{0:T(1024)S(1)}, u32[]{:S(2)}) copy-start(f32[768]{0:T(1024)S(1)} %get-tuple-element.73) | copy-start | bytes 9220
  41.6 2.1 copy-start.9
  41.6 2.1 copy-start.13
  54.1 2.1 collective-permute-start.3
  57.8 2.0 copy-start.32
  60.5 2.8 copy-start.30
  65.4 12.4 %collective-permute-start.6 = (bf16[1,128,768]{2,1,0:T(8,128)(2,1)}, bf16[1,128,768]{2,1,0:T(8,128)(2,1)}, u32[]{:S(2)}, u32[]{:S(2)}) collective-permute-start(bf16[1,128,768]{2,1,0:T(8,128)(2,1)} %get-tuple-element.43), channel_id=1, source_target_pairs={{0,1},{2,3},{4,5},{6,7},{8,9},{10,11},{12,13},{14,15},{16,17},{18,... | collective-permute-start | bytes 589832 | tf_op jit(solution)/shard_map/ppermute | solution.py:14
  68.3 7.5 collective-permute-start.4
  71.3 13.6 %collective-permute-start.5 = (bf16[1,128,768]{2,1,0:T(8,128)(2,1)}, bf16[1,128,768]{2,1,0:T(8,128)(2,1)}, u32[]{:S(2)}, u32[]{:S(2)}) collective-permute-start(bf16[1,128,768]{2,1,0:T(8,128)(2,1)} %get-tuple-element.45), channel_id=1, source_target_pairs={{0,1},{2,3},{4,5},{6,7},{8,9},{10,11},{12,13},{14,15},{16,17},{18,... | collective-permute-start | bytes 589832 | tf_op jit(solution)/shard_map/ppermute | solution.py:14
  81.6 3.3 copy-start.22
  88.5 2.2 copy-start.4
  88.5 2.2 copy-start.10
  91.1 11.5 %copy-start.7 = (f32[128,768]{1,0:T(8,128)}, f32[128,768]{1,0:T(8,128)S(1)}, u32[]{:S(2)}) copy-start(f32[128,768]{1,0:T(8,128)S(1)} %get-tuple-element.64) | copy-start | bytes 1179652
  91.2 11.5 %copy-start.40 = (f32[128]{0:T(128)}, f32[128]{0:T(128)S(1)}, u32[]{:S(2)}) copy-start(f32[128]{0:T(128)S(1)} %broadcast_multiply_fusion.1) | copy-start | bytes 1540
  91.4 11.3 %copy-start.47 = (f32[128]{0:T(128)}, f32[128]{0:T(128)S(1)}, u32[]{:S(2)}) copy-start(f32[128]{0:T(128)S(1)} %fusion.112) | copy-start | bytes 1540
  91.4 3.4 copy-start.17
  91.4 8.9 slice-start
  94.8 5.5 copy-start.11
  94.8 5.5 slice-start.1
  100.3 2.3 copy-start.18
  109.2 226.1 %reduce-scatter.8.cloned.1.call-start = ((), (), s32[]{:S(2)}) async-start(), calls=%async_computation.6 | async-start | bytes 7299072 | tf_op jit(solution)/shard_map/reduce_scatter | solution.py:343
  113.6 2.5 copy-start.2
  117.0 1.7 copy-start.19
  117.3 3.4 copy-start.16
  117.3 3.9 collective-permute-start.7
  119.3 4.3 copy-start.5
  119.3 4.3 copy-start.34
  119.3 4.2 copy-start.45
  119.3 4.2 copy-start.49
  119.3 3.5 collective-permute-start.8
  135.0 341.5 %reduce-scatter.12.cloned.1.call-start = ((), (), s32[]{:S(2)}) async-start(), calls=%async_computation.10 | async-start | bytes 9732096 | tf_op jit(solution)/shard_map/reduce_scatter | solution.py:345
  151.4 466.6 %reduce-scatter.14.cloned.1.call-start = ((), (), s32[]{:S(2)}) async-start(), calls=%async_computation.12 | async-start | bytes 9732096 | tf_op jit(solution)/shard_map/reduce_scatter | solution.py:346
  167.6 455.4 %copy-start.46 = (f32[128]{0:T(128)S(1)}, f32[128]{0:T(128)}, u32[]{:S(2)}) copy-start(f32[128]{0:T(128)} %copy-done.44) | copy-start | bytes 1540
  167.6 455.4 %copy-start.50 = (f32[128]{0:T(128)S(1)}, f32[128]{0:T(128)}, u32[]{:S(2)}) copy-start(f32[128]{0:T(128)} %copy-done.48) | copy-start | bytes 1540
  167.6 562.3 %all-gather.7.cloned.1.call-start = ((), (), s32[]{:S(2)}) async-start(), calls=%async_computation.9 | async-start | bytes 1216512 | tf_op jit(solution)/shard_map/all_gather | solution.py:352
  211.9 530.7 %all-gather.5.cloned.1.call-start = ((), (), s32[]{:S(2)}) async-start(), calls=%async_computation.7 | async-start | bytes 3649536 | tf_op jit(solution)/shard_map/all_gather | solution.py:349
  336.9 476.9 %all-gather.9.cloned.1.call-start = ((), (), s32[]{:S(2)}) async-start(), calls=%async_computation.11 | async-start | bytes 4866048 | tf_op jit(solution)/shard_map/all_gather | solution.py:355
  478.2 401.0 %all-gather.11.cloned.1.call-start = ((), (), s32[]{:S(2)}) async-start(), calls=%async_computation.13 | async-start | bytes 4866048 | tf_op jit(solution)/shard_map/all_gather | solution.py:358
  619.7 391.1 %all-reduce.5.cloned.1.call-start = ((), (), s32[]{:S(2)}) async-start(), calls=%async_computation.14 | async-start | bytes 884736 | tf_op jit(solution)/shard_map/psum | solution.py:325
  623.0 3.4 copy-start.56
  623.0 3.4 copy-start.6
  623.0 3.6 copy-start.15
  633.0 377.8 %reduce-scatter.6.cloned.1.call-start = ((), (), s32[]{:S(2)}) async-start(), calls=%async_computation.5 | async-start | bytes 3342336 | tf_op jit(solution)/shard_map/reduce_scatter | solution.py:312
  635.0 46.0 %copy-start.31 = (bf16[1,128,96]{1,2,0:T(8,128)(2,1)S(1)}, bf16[1,128,96]{1,2,0:T(8,128)(2,1)}, u32[]{:S(2)}) copy-start(bf16[1,128,96]{1,2,0:T(8,128)(2,1)} %copy-done.30) | copy-start | bytes 73732
  635.0 47.5 %copy-start.43 = (f32[768]{0:T(1024)S(1)}, f32[768]{0:T(1024)}, u32[]{:S(2)}) copy-start(f32[768]{0:T(1024)} %get-tuple-element.19) | copy-start | bytes 9220
  635.0 47.5 %copy-start.42 = (f32[768]{0:T(1024)S(1)}, f32[768]{0:T(1024)}, u32[]{:S(2)}) copy-start(f32[768]{0:T(1024)} %get-tuple-element.23) | copy-start | bytes 9220
  635.0 47.5 %copy-start.52 = (f32[768]{0:T(1024)S(1)}, f32[768]{0:T(1024)}, u32[]{:S(2)}) copy-start(f32[768]{0:T(1024)} %get-tuple-element.21) | copy-start | bytes 9220
  635.0 47.5 %copy-start.51 = (f32[768]{0:T(1024)S(1)}, f32[768]{0:T(1024)}, u32[]{:S(2)}) copy-start(f32[768]{0:T(1024)} %get-tuple-element.24) | copy-start | bytes 9220
  635.0 11.8 %collective-permute-start.9 = (f32[128,768]{1,0:T(8,128)}, f32[128,768]{1,0:T(8,128)S(1)}, u32[]{:S(2)}, u32[]{:S(2)}) collective-permute-start(f32[128,768]{1,0:T(8,128)} %get-tuple-element.36), channel_id=1, source_target_pairs={{0,2},{2,0},{4,6},{6,4},{8,10},{10,8},{12,14},{14,12},{16,18},{18,... | collective-permute-start | bytes 1179656 | tf_op jit(solution)/shard_map/ppermute | solution.py:315
  647.9 10.4 %collective-permute-start.10 = (f32[128,768]{1,0:T(8,128)S(1)}, f32[128,768]{1,0:T(8,128)S(1)}, u32[]{:S(2)}, u32[]{:S(2)}) collective-permute-start(f32[128,768]{1,0:T(8,128)S(1)} %add.293), channel_id=1, source_target_pairs={{0,4},{2,6},{4,0},{6,2},{8,12},{10,14},{12,8},{14,10},{16,20},{18,... | collective-permute-start | bytes 1179656 | tf_op jit(solution)/shard_map/ppermute | solution.py:315
  658.3 18.2 %collective-permute-start.11 = (f32[128,768]{1,0:T(8,128)S(1)}, f32[128,768]{1,0:T(8,128)S(1)}, u32[]{:S(2)}, u32[]{:S(2)}) collective-permute-start(f32[128,768]{1,0:T(8,128)S(1)} %add.294), channel_id=1, source_target_pairs={{0,8},{2,10},{4,12},{6,14},{8,0},{10,2},{12,4},{14,6},{16,24},{18,... | collective-permute-start | bytes 1179656 | tf_op jit(solution)/shard_map/ppermute | solution.py:315
  677.3 50.7 %collective-permute-start.12 = (f32[128,768]{1,0:T(8,128)}, f32[128,768]{1,0:T(8,128)}, u32[]{:S(2)}, u32[]{:S(2)}) collective-permute-start(f32[128,768]{1,0:T(8,128)} %add.295), channel_id=1, source_target_pairs={{0,16},{2,18},{4,20},{6,22},{8,24},{10,26},{12,28},{14,30},{16,0},... | collective-permute-start | bytes 1179656 | tf_op jit(solution)/shard_map/ppermute | solution.py:315
  (20 other events, 18.9 us)
Sparse Core Ops, SparseCore 0:
  109.3 101.0 reduce-scatter.9
  217.0 118.1 reduce-scatter.7
  341.7 134.7 reduce-scatter.11
  483.3 134.7 reduce-scatter.13
  620.8 56.8 all-gather.6
  681.0 61.6 all-gather.4
  746.2 67.5 all-gather.8
  816.6 62.4 all-gather.10
  885.7 125.0 all-reduce.4
Sparse Core Ops, SparseCore 1:
  639.8 148.1 reduce-scatter.5
